TPU v7x, 32 devices: a whole 2x2x4 slice. The times are simulated.
32 devices in a mesh: dp: 8 (over z, y), mp: 4 (over x, core).
Axes of the slice: x: 2, y: 2, z: 4, core: 2. Of those that a mesh axis runs over, the one named last changes fastest.
Arguments:
- tokens: bfloat16 [4096, 2048], P('dp'), may hold values from -6 to 6
- text: bfloat16 [2048, 4096], P('dp', 'mp'), may hold values from -6 to 6
- image_seg: int32 [8, 512], P('dp'), may hold values from 0 to 1, never falling along the last dimension, each value on 1 to 320 neighbouring positions
- text_seg: int32 [8, 256], P('dp'), may hold values from 0 to 1, never falling along the last dimension, each value on 1 to 160 neighbouring positions
- w_qkv: bfloat16 [3, 2048, 2048], P(None, 'dp', 'mp'), may hold values from -0.125 to 0.125
- w_out: bfloat16 [2048, 2048], P('mp', 'dp'), may hold values from -1 to 1
- c_q: bfloat16 [2048, 2048], P('dp', 'mp'), may hold values from -0.125 to 0.125
- c_kv: bfloat16 [2, 4096, 2048], P(None, 'dp', 'mp'), may hold values from -0.09375 to 0.09375
- c_out: bfloat16 [2048, 2048], P('mp', 'dp'), may hold values from -1 to 1
- w_up: bfloat16 [2048, 8192], P('dp', 'mp'), may hold values from -0.125 to 0.125
- w_down: bfloat16 [8192, 2048], P('mp', 'dp'), may hold values from -0.0625 to 0.0625
- norm_gain: float32 [4, 2048], replicated, may hold values from 0.25 to 1.75
- norm_bias: float32 [4, 2048], replicated, may hold values from -4 to 4
- out_bias: float32 [3, 2048], replicated, may hold values from -4 to 4
- up_bias: float32 [8192], P('mp'), may hold values from -4 to 4
- cotangent: bfloat16 [4096, 2048], P('dp'), may hold values from -6 to 6
Outputs:
- output: bfloat16 [4096, 2048], P('dp')
- grad_tokens: float32 [4096, 2048], P('dp')
- grad_text: float32 [2048, 4096], P('dp', 'mp')
- grad_w_qkv: float32 [3, 2048, 2048], P(None, 'dp', 'mp')
- grad_w_out: float32 [2048, 2048], P('mp', 'dp')
- grad_c_q: float32 [2048, 2048], P('dp', 'mp')
- grad_c_kv: float32 [2, 4096, 2048], P(None, 'dp', 'mp')
- grad_c_out: float32 [2048, 2048], P('mp', 'dp')
- grad_w_up: float32 [2048, 8192], P('dp', 'mp')
- grad_w_down: float32 [8192, 2048], P('mp', 'dp')
- grad_norm_gain: float32 [4, 2048], replicated
- grad_norm_bias: float32 [4, 2048], replicated
- grad_out_bias: float32 [3, 2048], replicated
- grad_up_bias: float32 [8192], P('mp')
Inputs may be any that keep to these rules, and one draw needn't show every extreme that they name: In each row image_seg is 0 on the first image and 1 on the second; both images are present, and none has more than 320 tokens. In each row text_seg is 0 on the first caption and 1 on the second; both captions are present, and none has more than 160 tokens.
All inputs are finite; a program needn't handle non-finite values.
Results may differ from a plain program's by a relative error of at most 0.02.
Values may be sent and summed in bfloat16 or wider, within the bound.
No kernel may reach another device: no remote copies, remote signals or barrier semaphores. Data moves between devices by JAX's collectives and lax.ppermute only.
A program may use at most 256 MiB of HBM per device.

v0:
```python
import jax
import jax.numpy as jnp
from jax import lax
from jax.sharding import PartitionSpec as P

HD = 128
eps = 1e-05
masked = -1e30


def normalize(values, gain, shift):
    center = values - jnp.mean(values, axis=-1, keepdims=True)
    spread = jnp.mean(center * center, axis=-1, keepdims=True)
    return center * lax.rsqrt(spread + eps) * gain + shift


def gelu_tanh(values):
    return (
        0.5
        * values
        * (1.0 + jnp.tanh(0.7978845608028654 * (values + 0.044715 * values * values * values)))
    )


def heads_sum(partial_value):
    return lax.psum(partial_value, "mp")


def input_sum(partial_value):
    return lax.psum(partial_value, "mp")


def split_heads(values):
    return values.reshape(values.shape[0], values.shape[1] // HD, HD)


def scores_of(queries, key_rows, allowed):
    raw = jnp.einsum(
        "qhd,khd->hqk",
        split_heads(queries),
        split_heads(key_rows),
        preferred_element_type=jnp.float32,
    ) * HD ** (-0.5)
    return jnp.where(allowed[None], raw, masked)


def attend_forward(queries, key_rows, value_rows, allowed):
    scores = scores_of(queries, key_rows, allowed)
    top = jnp.max(scores, axis=-1, keepdims=True)
    expo = jnp.exp(scores - top)
    total = jnp.sum(expo, axis=-1, keepdims=True)
    probs = (expo / total).astype(jnp.bfloat16)
    mixed = jnp.einsum(
        "hqk,khd->qhd", probs, split_heads(value_rows), preferred_element_type=jnp.float32
    )
    return (
        mixed.reshape(queries.shape[0], queries.shape[1]).astype(jnp.bfloat16),
        top + jnp.log(total),
    )


def attend_backward(queries, key_rows, value_rows, grad_mixed, logsum, allowed):
    scores = scores_of(queries, key_rows, allowed)
    probs = jnp.exp(scores - logsum)
    grad_heads = split_heads(grad_mixed)
    grad_values = jnp.einsum(
        "hqk,qhd->khd", probs.astype(jnp.bfloat16), grad_heads, preferred_element_type=jnp.float32
    )
    grad_probs = jnp.einsum(
        "qhd,khd->hqk", grad_heads, split_heads(value_rows), preferred_element_type=jnp.float32
    )
    grad_scores = (
        probs * (grad_probs - jnp.sum(probs * grad_probs, axis=-1, keepdims=True))
    ).astype(jnp.bfloat16)
    grad_queries = jnp.einsum(
        "hqk,khd->qhd", grad_scores, split_heads(key_rows), preferred_element_type=jnp.float32
    ) * HD ** (-0.5)
    grad_keys = jnp.einsum(
        "hqk,qhd->khd", grad_scores, split_heads(queries), preferred_element_type=jnp.float32
    ) * HD ** (-0.5)
    return (
        grad_queries.reshape(queries.shape),
        grad_keys.reshape(key_rows.shape),
        grad_values.reshape(value_rows.shape),
    )


def on_device(
    tokens,
    text,
    image_seg,
    text_seg,
    w_qkv,
    w_out,
    c_q,
    c_kv,
    c_out,
    w_up,
    w_down,
    norm_gain,
    norm_bias,
    out_bias,
    up_bias,
    cotangent,
):
    row_count = image_seg.shape[0]
    length = image_seg.shape[1]
    text_len = text_seg.shape[1]
    gathered = (
        lax.all_gather(w_qkv, "dp", axis=1, tiled=True),
        lax.all_gather(w_out, "dp", axis=1, tiled=True),
        lax.all_gather(c_q, "dp", axis=0, tiled=True),
        lax.all_gather(c_kv, "dp", axis=1, tiled=True),
        lax.all_gather(c_out, "dp", axis=1, tiled=True),
        lax.all_gather(w_up, "dp", axis=0, tiled=True),
        lax.all_gather(w_down, "dp", axis=1, tiled=True),
    )
    full_qkv, full_out, full_cq, full_ckv, full_cout, full_up, full_down = gathered
    words = lax.all_gather(text, "mp", axis=1, tiled=True)
    same_image = image_seg[:, :, None] == image_seg[:, None, :]
    caption = image_seg[:, :, None] == text_seg[:, None, :]
    residual = tokens.astype(jnp.float32)
    width = full_qkv.shape[2]
    normed_one, pull_one = jax.vjp(normalize, residual, norm_gain[0], norm_bias[0])
    hidden_one = normed_one.astype(jnp.bfloat16)
    projected = jnp.einsum(
        "td,cde->cte", hidden_one, full_qkv, preferred_element_type=jnp.float32
    ).astype(jnp.bfloat16)
    self_inputs = (
        projected[0].reshape(row_count, length, width),
        projected[1].reshape(row_count, length, width),
        projected[2].reshape(row_count, length, width),
    )
    self_mixed, self_logsum = lax.map(
        lambda pieces: attend_forward(*pieces), self_inputs + (same_image,)
    )
    self_flat = self_mixed.reshape(row_count * length, width)
    after_self = (
        residual
        + heads_sum(jnp.dot(self_flat, full_out, preferred_element_type=jnp.float32))
        + out_bias[0]
    )
    normed_two, pull_two = jax.vjp(normalize, after_self, norm_gain[1], norm_bias[1])
    hidden_two = normed_two.astype(jnp.bfloat16)
    cross_query = jnp.dot(hidden_two, full_cq, preferred_element_type=jnp.float32).astype(
        jnp.bfloat16
    )
    text_kv = jnp.einsum("td,cde->cte", words, full_ckv, preferred_element_type=jnp.float32).astype(
        jnp.bfloat16
    )
    cross_inputs = (
        cross_query.reshape(row_count, length, width),
        text_kv[0].reshape(row_count, text_len, width),
        text_kv[1].reshape(row_count, text_len, width),
    )
    cross_mixed, cross_logsum = lax.map(
        lambda pieces: attend_forward(*pieces), cross_inputs + (caption,)
    )
    cross_flat = cross_mixed.reshape(row_count * length, width)
    after_cross = (
        after_self
        + heads_sum(jnp.dot(cross_flat, full_cout, preferred_element_type=jnp.float32))
        + out_bias[1]
    )
    normed_three, pull_three = jax.vjp(normalize, after_cross, norm_gain[2], norm_bias[2])
    hidden_three = normed_three.astype(jnp.bfloat16)
    pre_act = jnp.dot(hidden_three, full_up, preferred_element_type=jnp.float32) + up_bias
    activated, pull_gelu = jax.vjp(gelu_tanh, pre_act)
    act_low = activated.astype(jnp.bfloat16)
    after_mlp = (
        after_cross
        + heads_sum(jnp.dot(act_low, full_down, preferred_element_type=jnp.float32))
        + out_bias[2]
    )
    final, pull_four = jax.vjp(normalize, after_mlp, norm_gain[3], norm_bias[3])
    output = final.astype(jnp.bfloat16)
    grad_mlp, gain_four, shift_four = pull_four(cotangent.astype(jnp.float32))
    grad_mlp_low = grad_mlp.astype(jnp.bfloat16)
    grad_down = jnp.einsum("tf,td->fd", act_low, grad_mlp_low, preferred_element_type=jnp.float32)
    grad_act = jnp.einsum("td,fd->tf", grad_mlp_low, full_down, preferred_element_type=jnp.float32)
    grad_pre = pull_gelu(grad_act)[0].astype(jnp.bfloat16)
    up_bias_grad = jnp.sum(grad_pre.astype(jnp.float32), axis=0)
    grad_up = jnp.einsum("td,tf->df", hidden_three, grad_pre, preferred_element_type=jnp.float32)
    grad_hidden_three = input_sum(
        jnp.einsum("tf,df->td", grad_pre, full_up, preferred_element_type=jnp.float32)
    )
    grad_cross_in, gain_three, shift_three = pull_three(grad_hidden_three)
    grad_after_cross = grad_mlp + grad_cross_in
    grad_cross_low = grad_after_cross.astype(jnp.bfloat16)
    grad_cout = jnp.einsum(
        "te,td->ed", cross_flat, grad_cross_low, preferred_element_type=jnp.float32
    )
    grad_cmix = jnp.einsum(
        "td,ed->te", grad_cross_low, full_cout, preferred_element_type=jnp.float32
    ).astype(jnp.bfloat16)
    cq_grad, ck_grad, cv_grad = lax.map(
        lambda pieces: attend_backward(*pieces),
        cross_inputs + (grad_cmix.reshape(row_count, length, width), cross_logsum, caption),
    )
    cq_low = cq_grad.reshape(row_count * length, width).astype(jnp.bfloat16)
    ckv_low = jnp.stack(
        [ck_grad.reshape(row_count * text_len, width), cv_grad.reshape(row_count * text_len, width)]
    ).astype(jnp.bfloat16)
    grad_cq = jnp.einsum("td,te->de", hidden_two, cq_low, preferred_element_type=jnp.float32)
    grad_ckv = jnp.einsum("td,cte->cde", words, ckv_low, preferred_element_type=jnp.float32)
    text_term = jnp.einsum("cte,cde->td", ckv_low, full_ckv, preferred_element_type=jnp.float32)
    grad_text = lax.psum_scatter(
        text_term.astype(jnp.bfloat16), "mp", scatter_dimension=1, tiled=True
    ).astype(jnp.float32)
    grad_hidden_two = input_sum(
        jnp.einsum("te,de->td", cq_low, full_cq, preferred_element_type=jnp.float32)
    )
    grad_self_in, gain_two, shift_two = pull_two(grad_hidden_two)
    grad_after_self = grad_after_cross + grad_self_in
    grad_self_low = grad_after_self.astype(jnp.bfloat16)
    grad_wout = jnp.einsum(
        "te,td->ed", self_flat, grad_self_low, preferred_element_type=jnp.float32
    )
    grad_smix = jnp.einsum(
        "td,ed->te", grad_self_low, full_out, preferred_element_type=jnp.float32
    ).astype(jnp.bfloat16)
    sq_grad, sk_grad, sv_grad = lax.map(
        lambda pieces: attend_backward(*pieces),
        self_inputs + (grad_smix.reshape(row_count, length, width), self_logsum, same_image),
    )
    qkv_low = jnp.stack(
        [
            sq_grad.reshape(row_count * length, width),
            sk_grad.reshape(row_count * length, width),
            sv_grad.reshape(row_count * length, width),
        ]
    ).astype(jnp.bfloat16)
    grad_qkv = jnp.einsum("td,cte->cde", hidden_one, qkv_low, preferred_element_type=jnp.float32)
    grad_hidden_one = input_sum(
        jnp.einsum("cte,cde->td", qkv_low, full_qkv, preferred_element_type=jnp.float32)
    )
    grad_in_one, gain_one, shift_one = pull_one(grad_hidden_one)
    grad_tokens = grad_after_self + grad_in_one
    gain_terms = jnp.stack([gain_one, gain_two, gain_three, gain_four])
    shift_terms = jnp.stack([shift_one, shift_two, shift_three, shift_four])
    bias_terms = jnp.stack(
        [
            jnp.sum(grad_after_self, axis=0),
            jnp.sum(grad_after_cross, axis=0),
            jnp.sum(grad_mlp, axis=0),
        ]
    )
    gain_total, shift_total, bias_total, up_total = (
        lax.psum(gain_terms.astype(jnp.bfloat16), "dp").astype(jnp.float32),
        lax.psum(shift_terms.astype(jnp.bfloat16), "dp").astype(jnp.float32),
        lax.psum(bias_terms.astype(jnp.bfloat16), "dp").astype(jnp.float32),
        lax.psum(up_bias_grad.astype(jnp.bfloat16), "dp").astype(jnp.float32),
    )
    sum_qkv, sum_wout, sum_cq, sum_ckv, sum_cout, sum_up, sum_down = (
        lax.psum_scatter(
            grad_qkv.astype(jnp.bfloat16), "dp", scatter_dimension=1, tiled=True
        ).astype(jnp.float32),
        lax.psum_scatter(
            grad_wout.astype(jnp.bfloat16), "dp", scatter_dimension=1, tiled=True
        ).astype(jnp.float32),
        lax.psum_scatter(
            grad_cq.astype(jnp.bfloat16), "dp", scatter_dimension=0, tiled=True
        ).astype(jnp.float32),
        lax.psum_scatter(
            grad_ckv.astype(jnp.bfloat16), "dp", scatter_dimension=1, tiled=True
        ).astype(jnp.float32),
        lax.psum_scatter(
            grad_cout.astype(jnp.bfloat16), "dp", scatter_dimension=1, tiled=True
        ).astype(jnp.float32),
        lax.psum_scatter(
            grad_up.astype(jnp.bfloat16), "dp", scatter_dimension=0, tiled=True
        ).astype(jnp.float32),
        lax.psum_scatter(
            grad_down.astype(jnp.bfloat16), "dp", scatter_dimension=1, tiled=True
        ).astype(jnp.float32),
    )
    return (
        output,
        grad_tokens,
        grad_text,
        sum_qkv,
        sum_wout,
        sum_cq,
        sum_ckv,
        sum_cout,
        sum_up,
        sum_down,
        gain_total,
        shift_total,
        bias_total,
        up_total,
    )


def solution(mesh):
    in_specs = (
        P("dp", None),
        P("dp", "mp"),
        P("dp", None),
        P("dp", None),
        P(None, "dp", "mp"),
        P("mp", "dp"),
        P("dp", "mp"),
        P(None, "dp", "mp"),
        P("mp", "dp"),
        P("dp", "mp"),
        P("mp", "dp"),
        P(),
        P(),
        P(),
        P("mp"),
        P("dp", None),
    )
    out_specs = (
        P("dp", None),
        P("dp", None),
        P("dp", "mp"),
        P(None, "dp", "mp"),
        P("mp", "dp"),
        P("dp", "mp"),
        P(None, "dp", "mp"),
        P("mp", "dp"),
        P("dp", "mp"),
        P("mp", "dp"),
        P(),
        P(),
        P(),
        P("mp"),
    )
    return jax.shard_map(
        on_device, mesh=mesh, in_specs=in_specs, out_specs=out_specs, check_vma=False
    )
```

profile of v0, /device:TPU:0, one launch (start us, length us, event | category | flops | bytes accessed | tf_op | source)
XLA Modules:
  0.0 2109.8 jit_solution(6485817762568258638)
XLA Ops:
  13.9 99.0 %all-gather.9.cloned.1.call-done = bf16[3,2048,512]{1,2,0:T(8,128)(2,1)} async-done(((bf16[3,256,512]{1,2,0:T(8,128)(2,1)}), bf16[3,2048,512]{1,2,0:T(8,128)(2,1)}) %all-gather.9.cloned.1.call-update) | async-done | bytes 6291472 | tf_op jit(solution)/shard_map/all_gather | solution.py:110
  124.3 39.2 %all-gather.11.cloned.1.call-done = bf16[512,2048]{1,0:T(8,128)(2,1)} async-done(((bf16[512,256]{1,0:T(8,128)(2,1)}), bf16[512,2048]{1,0:T(8,128)(2,1)}) %all-gather.11.cloned.1.call-update) | async-done | bytes 2097168 | tf_op jit(solution)/shard_map/all_gather | solution.py:111
  172.5 79.7 %all-reduce.8.cloned.1.call-done = f32[512,2048]{1,0:T(8,128)} async-done(((f32[512,2048]{1,0:T(8,128)}), f32[512,2048]{1,0:T(8,128)}) %all-reduce.8.cloned.1.call-update) | async-done | bytes 4194320 | tf_op jit(solution)/shard_map/psum | solution.py:26
  257.8 45.6 %all-gather.17.cloned.1.call-done = bf16[2048,512]{1,0:T(8,128)(2,1)} async-done(((bf16[256,512]{1,0:T(8,128)(2,1)}), bf16[2048,512]{1,0:T(8,128)(2,1)}) %all-gather.17.cloned.1.call-update) | async-done | bytes 2097168 | tf_op jit(solution)/shard_map/all_gather | solution.py:112
  306.4 19.6 all-gather.15.cloned.1.call-done
  326.0 127.4 %all-gather.13.cloned.1.call-done = bf16[2,4096,512]{1,2,0:T(8,128)(2,1)} async-done(((bf16[2,512,512]{1,2,0:T(8,128)(2,1)}), bf16[2,4096,512]{1,2,0:T(8,128)(2,1)}) %all-gather.13.cloned.1.call-update) | async-done | bytes 8388624 | tf_op jit(solution)/shard_map/all_gather | solution.py:113
  461.3 42.8 %all-gather.19.cloned.1.call-done = bf16[512,2048]{1,0:T(8,128)(2,1)} async-done(((bf16[512,256]{1,0:T(8,128)(2,1)}), bf16[512,2048]{1,0:T(8,128)(2,1)}) %all-gather.19.cloned.1.call-update) | async-done | bytes 2097168 | tf_op jit(solution)/shard_map/all_gather | solution.py:114
  510.5 82.3 %all-reduce.10.cloned.1.call-done = f32[512,2048]{1,0:T(8,128)} async-done(((f32[512,2048]{1,0:T(8,128)}), f32[512,2048]{1,0:T(8,128)}) %all-reduce.10.cloned.1.call-update) | async-done | bytes 4194320 | tf_op jit(solution)/shard_map/psum | solution.py:26
  599.3 120.2 %all-gather.21.cloned.1.call-done = bf16[2048,2048]{1,0:T(8,128)(2,1)} async-done(((bf16[256,2048]{1,0:T(8,128)(2,1)}), bf16[2048,2048]{1,0:T(8,128)(2,1)}) %all-gather.21.cloned.1.call-update) | async-done | bytes 8388624 | tf_op jit(solution)/shard_map/all_gather | solution.py:115
  719.5 11.2 fusion.69
  730.7 113.8 %all-gather.23.cloned.1.call-done = bf16[2048,2048]{1,0:T(8,128)(2,1)} async-done(((bf16[2048,256]{1,0:T(8,128)(2,1)}), bf16[2048,2048]{1,0:T(8,128)(2,1)}) %all-gather.23.cloned.1.call-update) | async-done | bytes 8388624 | tf_op jit(solution)/shard_map/all_gather | solution.py:116
  844.5 11.5 fusion.68
  856.4 83.6 %all-reduce.12.cloned.1.call-done = f32[512,2048]{1,0:T(8,128)} async-done(((f32[512,2048]{1,0:T(8,128)}), f32[512,2048]{1,0:T(8,128)}) %all-reduce.12.cloned.1.call-update) | async-done | bytes 4194320 | tf_op jit(solution)/shard_map/psum | solution.py:26
  950.0 12.0 fusion.87
  969.7 85.5 %all-reduce.14.cloned.1.call-done = f32[512,2048]{1,0:T(8,128)} async-done(((f32[512,2048]{1,0:T(8,128)}), f32[512,2048]{1,0:T(8,128)}) %all-reduce.14.cloned.1.call-update) | async-done | bytes 4194320 | tf_op jit(solution)/shard_map/psum | solution.py:30
  1072.5 85.2 %all-reduce.16.cloned.1.call-done = f32[512,2048]{1,0:T(8,128)} async-done(((f32[512,2048]{1,0:T(8,128)}), f32[512,2048]{1,0:T(8,128)}) %all-reduce.16.cloned.1.call-update) | async-done | bytes 4194320 | tf_op jit(solution)/shard_map/psum | solution.py:30
  1183.2 8.6 convolution_bitcast_fusion.1
  1201.5 7.2 fusion.4
  1218.7 12.4 convolution_convert_fusion
  1232.7 9.4 convolution_convert_fusion.1
  1244.1 7.1 convert_bitcast_fusion.1
  1251.2 7.2 convert_bitcast_fusion
  1260.7 16.9 all-reduce.18.cloned.1.call-done
  1283.1 38.6 %all-reduce = (bf16[4,2048]{1,0:T(4,128)(2,1)S(1)}, bf16[4,2048]{1,0:T(4,128)(2,1)S(1)}, bf16[3,2048]{1,0:T(4,128)(2,1)S(1)}, bf16[2048]{0:T(1024)(128)(2,1)S(1)}) all-reduce(bf16[4,2048]{1,0:T(4,128)(2,1)S(1)} %get-tuple-element.190, bf16[4,2048]{1,0:T(4,128)(2,1)S(1)} %get-tuple-element.191, ...), channel_id=1, replica_groups=mesh['dp'=8,'mp'=4] {'dp'}, use_global_device_ids=true, to_apply=%region_40.41 | all-reduce | flops 24576 | bytes 98304 | tf_op jit(solution)/shard_map/psum | solution.py:249
  1329.8 20.3 reduce-scatter.15.cloned.1.call-done
  1352.0 31.5 %reduce-scatter.9.cloned.1.call-done = bf16[256,1024]{1,0:T(8,128)(2,1)} async-done(((bf16[256,4096]{1,0:T(8,128)(2,1)}), bf16[256,1024]{1,0:T(8,128)(2,1)}) %reduce-scatter.9.cloned.1.call-update) | async-done | bytes 524304 | tf_op jit(solution)/shard_map/reduce_scatter | solution.py:207
  1385.6 70.2 %reduce-scatter.19.cloned.1.call-done = bf16[512,256]{1,0:T(8,128)(2,1)} async-done(((bf16[512,2048]{1,0:T(8,128)(2,1)}), bf16[512,256]{1,0:T(8,128)(2,1)}) %reduce-scatter.19.cloned.1.call-update) | async-done | bytes 262160 | tf_op jit(solution)/shard_map/reduce_scatter | solution.py:267
  1457.5 70.0 %reduce-scatter.13.cloned.1.call-done = bf16[512,256]{1,0:T(8,128)(2,1)} async-done(((bf16[512,2048]{1,0:T(8,128)(2,1)}), bf16[512,256]{1,0:T(8,128)(2,1)}) %reduce-scatter.13.cloned.1.call-update) | async-done | bytes 262160 | tf_op jit(solution)/shard_map/reduce_scatter | solution.py:258
  1529.3 148.7 %reduce-scatter.23.cloned.1.call-done = bf16[2048,256]{1,0:T(8,128)(2,1)} async-done(((bf16[2048,2048]{1,0:T(8,128)(2,1)}), bf16[2048,256]{1,0:T(8,128)(2,1)}) %reduce-scatter.23.cloned.1.call-update) | async-done | bytes 1048592 | tf_op jit(solution)/shard_map/reduce_scatter | solution.py:273
  1680.8 147.4 %reduce-scatter.21.cloned.1.call-done = bf16[256,2048]{1,0:T(8,128)(2,1)} async-done(((bf16[2048,2048]{1,0:T(8,128)(2,1)}), bf16[256,2048]{1,0:T(8,128)(2,1)}) %reduce-scatter.21.cloned.1.call-update) | async-done | bytes 1048592 | tf_op jit(solution)/shard_map/reduce_scatter | solution.py:270
  1830.9 118.5 %reduce-scatter.11.cloned.1.call-done = bf16[3,256,512]{1,2,0:T(8,128)(2,1)} async-done(((bf16[3,2048,512]{1,2,0:T(8,128)(2,1)}), bf16[3,256,512]{1,2,0:T(8,128)(2,1)}) %reduce-scatter.11.cloned.1.call-update) | async-done | bytes 786448 | tf_op jit(solution)/shard_map/reduce_scatter | solution.py:255
  1951.9 148.2 %reduce-scatter.17.cloned.1.call-done = bf16[2,512,512]{1,2,0:T(8,128)(2,1)} async-done(((bf16[2,4096,512]{1,2,0:T(8,128)(2,1)}), bf16[2,512,512]{1,2,0:T(8,128)(2,1)}) %reduce-scatter.17.cloned.1.call-update) | async-done | bytes 1048592 | tf_op jit(solution)/shard_map/reduce_scatter | solution.py:264
  (265 shorter events, 173.4 us)
Async XLA Ops:
  7.2 105.7 %all-gather.9.cloned.1.call-start = ((), (), s32[]{:S(2)}) async-start(), calls=%async_computation.8 | async-start | bytes 7077888 | tf_op jit(solution)/shard_map/all_gather | solution.py:110
  9.7 153.8 %all-gather.11.cloned.1.call-start = ((), (), s32[]{:S(2)}) async-start(), calls=%async_computation.9 | async-start | bytes 2359296 | tf_op jit(solution)/shard_map/all_gather | solution.py:111
  10.5 241.7 %all-reduce.8.cloned.1.call-start = ((), (), s32[]{:S(2)}) async-start(), calls=%async_computation.10 | async-start | bytes 8388608 | tf_op jit(solution)/shard_map/psum | solution.py:26
  12.5 107.0 %copy-start.38 = (f32[512]{0:T(512)}, f32[512]{0:T(512)S(1)}, u32[]{:S(2)}) copy-start(f32[512]{0:T(512)S(1)} %broadcast_multiply_fusion.3) | copy-start | bytes 6148
  13.8 105.7 %copy-start.43 = (f32[512]{0:T(512)}, f32[512]{0:T(512)S(1)}, u32[]{:S(2)}) copy-start(f32[512]{0:T(512)S(1)} %fusion.58) | copy-start | bytes 6148
  13.8 105.7 %copy-start.36 = (f32[1,2048]{1,0:T(1,128)}, f32[1,2048]{1,0:T(1,128)S(1)}, u32[]{:S(2)}) copy-start(f32[1,2048]{1,0:T(1,128)S(1)} %get-tuple-element.171) | copy-start | bytes 24580
  13.9 105.6 %copy-start.48 = (f32[1,2048]{1,0:T(1,128)}, f32[1,2048]{1,0:T(1,128)S(1)}, u32[]{:S(2)}) copy-start(f32[1,2048]{1,0:T(1,128)S(1)} %get-tuple-element.175) | copy-start | bytes 24580
  124.3 39.2 %copy-start.32 = (bf16[4,128,512]{2,1,0:T(8,128)(2,1)}, bf16[4,128,512]{2,1,0:T(8,128)(2,1)S(1)}, u32[]{:S(2)}) copy-start(bf16[4,128,512]{2,1,0:T(8,128)(2,1)S(1)} %fusion.45) | copy-start | bytes 1572868
  168.4 135.1 %all-gather.17.cloned.1.call-start = ((), (), s32[]{:S(2)}) async-start(), calls=%async_computation.13 | async-start | bytes 2359296 | tf_op jit(solution)/shard_map/all_gather | solution.py:112
  169.0 157.0 %all-gather.15.cloned.1.call-start = ((), (), s32[]{:S(2)}) async-start(), calls=%async_computation.12 | async-start | bytes 2621440 | tf_op jit(solution)/shard_map/all_gather | solution.py:119
  169.6 283.9 %all-gather.13.cloned.1.call-start = ((), (), s32[]{:S(2)}) async-start(), calls=%async_computation.11 | async-start | bytes 9437184 | tf_op jit(solution)/shard_map/all_gather | solution.py:113
  171.0 333.1 %all-gather.19.cloned.1.call-start = ((), (), s32[]{:S(2)}) async-start(), calls=%async_computation.14 | async-start | bytes 2359296 | tf_op jit(solution)/shard_map/all_gather | solution.py:114
  171.7 421.0 %all-reduce.10.cloned.1.call-start = ((), (), s32[]{:S(2)}) async-start(), calls=%async_computation.15 | async-start | bytes 8388608 | tf_op jit(solution)/shard_map/psum | solution.py:26
  257.8 48.5 %copy-start.28 = (bf16[512,2048]{1,0:T(8,128)(2,1)}, bf16[512,2048]{1,0:T(8,128)(2,1)S(1)}, u32[]{:S(2)}) copy-start(bf16[512,2048]{1,0:T(8,128)(2,1)S(1)} %add_convert_fusion.2) | copy-start | bytes 6291460
  306.4 153.5 %copy-start.26 = (bf16[512,512]{0,1:T(8,128)(2,1)}, bf16[512,512]{0,1:T(8,128)(2,1)S(1)}, u32[]{:S(2)}) copy-start(bf16[512,512]{0,1:T(8,128)(2,1)S(1)} %convolution_convert_fusion.9) | copy-start | bytes 1572868
  461.3 47.6 %copy-start.34 = (bf16[4,128,512]{2,1,0:T(8,128)(2,1)}, bf16[4,128,512]{2,1,0:T(8,128)(2,1)S(1)}, u32[]{:S(2)}) copy-start(bf16[4,128,512]{2,1,0:T(8,128)(2,1)S(1)} %convolution_convert_fusion.8) | copy-start | bytes 1572868
  508.9 210.6 %all-gather.21.cloned.1.call-start = ((), (), s32[]{:S(2)}) async-start(), calls=%async_computation.16 | async-start | bytes 9437184 | tf_op jit(solution)/shard_map/all_gather | solution.py:115
  509.7 334.9 %all-gather.23.cloned.1.call-start = ((), (), s32[]{:S(2)}) async-start(), calls=%async_computation.17 | async-start | bytes 9437184 | tf_op jit(solution)/shard_map/all_gather | solution.py:116
  510.2 429.7 %all-reduce.12.cloned.1.call-start = ((), (), s32[]{:S(2)}) async-start(), calls=%async_computation.18 | async-start | bytes 8388608 | tf_op jit(solution)/shard_map/psum | solution.py:26
  719.5 125.0 %copy-start.51 = (f32[2048]{0:T(1024)S(1)}, f32[2048]{0:T(1024)}, u32[]{:S(2)}) copy-start(f32[2048]{0:T(1024)} %param.30) | copy-start | bytes 24580
  856.1 199.1 %all-reduce.14.cloned.1.call-start = ((), (), s32[]{:S(2)}) async-start(), calls=%async_computation.19 | async-start | bytes 8388608 | tf_op jit(solution)/shard_map/psum | solution.py:30
  969.4 188.3 %all-reduce.16.cloned.1.call-start = ((), (), s32[]{:S(2)}) async-start(), calls=%async_computation.20 | async-start | bytes 8388608 | tf_op jit(solution)/shard_map/psum | solution.py:30
  1071.9 205.7 %all-reduce.18.cloned.1.call-start = ((), (), s32[]{:S(2)}) async-start(), calls=%async_computation.21 | async-start | bytes 8388608 | tf_op jit(solution)/shard_map/psum | solution.py:30
  1191.8 158.3 %reduce-scatter.15.cloned.1.call-start = ((), (), s32[]{:S(2)}) async-start(), calls=%async_computation.25 | async-start | bytes 2359296 | tf_op jit(solution)/shard_map/reduce_scatter | solution.py:261
  1196.2 187.2 %reduce-scatter.9.cloned.1.call-start = ((), (), s32[]{:S(2)}) async-start(), calls=%async_computation.22 | async-start | bytes 2621440 | tf_op jit(solution)/shard_map/reduce_scatter | solution.py:207
  1208.7 247.0 %reduce-scatter.19.cloned.1.call-start = ((), (), s32[]{:S(2)}) async-start(), calls=%async_computation.27 | async-start | bytes 2359296 | tf_op jit(solution)/shard_map/reduce_scatter | solution.py:267
  1213.7 313.9 %reduce-scatter.13.cloned.1.call-start = ((), (), s32[]{:S(2)}) async-start(), calls=%async_computation.24 | async-start | bytes 2359296 | tf_op jit(solution)/shard_map/reduce_scatter | solution.py:258
  1218.6 459.5 %reduce-scatter.23.cloned.1.call-start = ((), (), s32[]{:S(2)}) async-start(), calls=%async_computation.29 | async-start | bytes 9437184 | tf_op jit(solution)/shard_map/reduce_scatter | solution.py:273
  1231.1 597.1 %reduce-scatter.21.cloned.1.call-start = ((), (), s32[]{:S(2)}) async-start(), calls=%async_computation.28 | async-start | bytes 9437184 | tf_op jit(solution)/shard_map/reduce_scatter | solution.py:270
  1242.2 707.2 %reduce-scatter.11.cloned.1.call-start = ((), (), s32[]{:S(2)}) async-start(), calls=%async_computation.23 | async-start | bytes 7077888 | tf_op jit(solution)/shard_map/reduce_scatter | solution.py:255
  1251.2 849.0 %reduce-scatter.17.cloned.1.call-start = ((), (), s32[]{:S(2)}) async-start(), calls=%async_computation.26 | async-start | bytes 9437184 | tf_op jit(solution)/shard_map/reduce_scatter | solution.py:264
  1258.5 22.4 %copy-start.47 = (f32[512]{0:T(512)S(1)}, f32[512]{0:T(512)}, u32[]{:S(2)}) copy-start(f32[512]{0:T(512)} %copy-done.46) | copy-start | bytes 6148
  (47 other events, 169.8 us)
Sparse Core Ops, SparseCore 0:
  10.6 102.1 all-gather.8
  114.9 48.5 all-gather.10
  168.5 83.6 all-reduce.7
  254.2 49.2 all-gather.16
  304.9 21.0 all-gather.14
  328.5 124.9 all-gather.12
  455.5 48.5 all-gather.18
  509.0 83.6 all-reduce.9
  594.9 124.6 all-gather.20
  721.4 123.1 all-gather.22
  856.2 83.6 all-reduce.11
  969.5 85.6 all-reduce.13
  1072.1 85.6 all-reduce.15
  1191.9 85.6 all-reduce.17
  1281.5 68.5 reduce-scatter.14
  1353.1 30.2 reduce-scatter.8
  1386.8 68.8 reduce-scatter.18
  1459.7 67.8 reduce-scatter.12
  1531.2 146.8 reduce-scatter.22
  1681.6 146.5 reduce-scatter.20
  1831.8 117.5 reduce-scatter.10
  1953.0 147.0 reduce-scatter.16
where the time goes:
time: 2120 us; the launch traced here: 2110 us
  waiting for transfers between devices  1800 us (85%)
  matrix products  151 us (7%)
  other arithmetic  65.1 us (3%)
  blocking collectives  38.6 us (2%)
  local copies, waits for them, and re-layouts  36.8 us (2%)
    psum x3, waiting for transfers between devices, heads_sum(): return lax.psum(partial_value, 'mp')  246 us
    psum x3, waiting for transfers between devices, input_sum(): return lax.psum(partial_value, 'mp')  188 us
    reduce_scatter x1, waiting for transfers between devices, on_device(): lax.psum_scatter(grad_down.astype(jnp.bfloat16), 'dp', scatter_dimension=...  149 us
    reduce_scatter x1, waiting for transfers between devices, on_device(): lax.psum_scatter(grad_ckv.astype(jnp.bfloat16), 'dp', scatter_dimension=1...  148 us
    reduce_scatter x1, waiting for transfers between devices, on_device(): lax.psum_scatter(grad_up.astype(jnp.bfloat16), 'dp', scatter_dimension=0,...  147 us
    all_gather x1, waiting for transfers between devices, on_device(): lax.all_gather(c_kv, 'dp', axis=1, tiled=True)  127 us
    all_gather x1, waiting for transfers between devices, on_device(): lax.all_gather(w_up, 'dp', axis=0, tiled=True)  120 us
    reduce_scatter x1, waiting for transfers between devices, on_device(): lax.psum_scatter(grad_qkv.astype(jnp.bfloat16), 'dp', scatter_dimension=1...  118 us
  transfers between devices with their start and end apart: 22, of which 22 were waited for; matrix products, arithmetic and copies ran while one was open for 7% of the time, Pallas kernels for 0%

commit v1 on v0

--- a/solution.py
+++ b/solution.py
@@ -1,3 +1,4 @@
+import functools
 import jax
 import jax.numpy as jnp
 from jax import lax
@@ -6,6 +7,34 @@
 HD = 128
 eps = 1e-05
 masked = -1e30
+
+
+def feed_the_field(buf, array_dim):
+    buf = jnp.moveaxis(buf, 0, array_dim)
+    base_arr = buf.shape
+    a_next = buf.reshape(
+        *base_arr[:array_dim],
+        base_arr[array_dim] * base_arr[array_dim + 1],
+        *base_arr[array_dim + 2 :]
+    )
+    return a_next
+
+
+def build_the_area(local, mesh_name, dim_at):
+    n_lanes = lax.axis_size(mesh_name)
+    pieces_in = [(src_i, (src_i + 1) % n_lanes) for src_i in range(n_lanes)]
+    chunks = [local]
+    while len(chunks) < n_lanes:
+        x_new = lax.ppermute(chunks[-1], axis_name=mesh_name, perm=pieces_in)
+        chunks.append(x_new)
+    res = lax.axis_index(mesh_name)
+    heard = jnp.stack(chunks, 0)
+    chunks = heard[(res - jnp.arange(n_lanes)) % n_lanes]
+    x_next = feed_the_field(chunks, dim_at)
+    return x_next
+
+
+column_trace = functools.partial(build_the_area, mesh_name="dp", dim_at=1)
 
 
 def normalize(values, gain, shift):
@@ -107,7 +136,7 @@
     length = image_seg.shape[1]
     text_len = text_seg.shape[1]
     gathered = (
-        lax.all_gather(w_qkv, "dp", axis=1, tiled=True),
+        column_trace(w_qkv),
         lax.all_gather(w_out, "dp", axis=1, tiled=True),
         lax.all_gather(c_q, "dp", axis=0, tiled=True),
         lax.all_gather(c_kv, "dp", axis=1, tiled=True),

time: 2120 us -> 2140 us (level)
    ppermute x0 -> x7, waiting for transfers between devices: none -> 142 us  [build_the_area(): x_new = lax.ppermute(chunks[-1], axis_name=mesh_name, perm=pieces_in)]
    all_gather x1 -> x0, waiting for transfers between devices: 99 us -> none  [on_device(): lax.all_gather(w_qkv, 'dp', axis=1, tiled=True)]
    all_gather x1, waiting for transfers between devices: 39.2 us -> 0.02 us  [on_device(): lax.all_gather(w_out, 'dp', axis=1, tiled=True)]
  transfers between devices with their start and end apart: 22 -> 28, of which waited for: 22 -> 27; matrix products, arithmetic and copies ran while one was open for 7% -> 7% of each run, Pallas kernels for 0% -> 0%
where the time goes in v1:
time: 2140 us; the launch traced here: 2130 us
  waiting for transfers between devices  1800 us (84%)
  matrix products  149 us (7%)
  other arithmetic  66.6 us (3%)
  local copies, waits for them, and re-layouts  53.5 us (2%)
  blocking collectives  38.9 us (2%)
    psum x3, waiting for transfers between devices, heads_sum(): return lax.psum(partial_value, 'mp')  244 us
    psum x3, waiting for transfers between devices, input_sum(): return lax.psum(partial_value, 'mp')  188 us
    reduce_scatter x1, waiting for transfers between devices, on_device(): lax.psum_scatter(grad_down.astype(jnp.bfloat16), 'dp', scatter_dimension=...  149 us
    reduce_scatter x1, waiting for transfers between devices, on_device(): lax.psum_scatter(grad_ckv.astype(jnp.bfloat16), 'dp', scatter_dimension=1...  148 us
    reduce_scatter x1, waiting for transfers between devices, on_device(): lax.psum_scatter(grad_up.astype(jnp.bfloat16), 'dp', scatter_dimension=0,...  148 us
    ppermute x7, waiting for transfers between devices, build_the_area(): x_new = lax.ppermute(chunks[-1], axis_name=mesh_name, perm=pieces_in)  142 us
    all_gather x1, waiting for transfers between devices, on_device(): lax.all_gather(c_kv, 'dp', axis=1, tiled=True)  127 us
    all_gather x1, waiting for transfers between devices, on_device(): lax.all_gather(w_up, 'dp', axis=0, tiled=True)  120 us
  transfers between devices with their start and end apart: 28, of which 27 were waited for; matrix products, arithmetic and copies ran while one was open for 7% of the time, Pallas kernels for 0%

profile of v1, /device:TPU:0, one launch (start us, length us, event | category | flops | bytes accessed | tf_op | source)
XLA Modules:
  0.0 2131.2 jit_solution(13360007467871900228)
XLA Ops:
  10.3 20.8 collective-permute-done
  31.2 27.5 %collective-permute-done.1 = bf16[3,256,512]{2,1,0:T(8,128)(2,1)S(1)} collective-permute-done((bf16[3,256,512]{2,1,0:T(8,128)(2,1)S(1)}, bf16[3,256,512]{2,1,0:T(8,128)(2,1)S(1)}, u32[]{:S(2)}, u32[]{:S(2)}) %collective-permute-start.1) | collective-permute-done | bytes 786464 | tf_op jit(solution)/shard_map/ppermute | solution.py:28
  62.9 15.1 collective-permute-done.2
  78.4 36.4 %collective-permute-done.3 = bf16[3,256,512]{2,1,0:T(8,128)(2,1)S(1)} collective-permute-done((bf16[3,256,512]{2,1,0:T(8,128)(2,1)}, bf16[3,256,512]{2,1,0:T(8,128)(2,1)S(1)}, u32[]{:S(2)}, u32[]{:S(2)}) %collective-permute-start.3) | collective-permute-done | bytes 786464 | tf_op jit(solution)/shard_map/ppermute | solution.py:28
  115.8 16.7 collective-permute-done.4
  136.4 13.8 collective-permute-done.5
  153.1 11.8 collective-permute-done.6
  193.9 78.6 %all-reduce.8.cloned.1.call-done = f32[512,2048]{1,0:T(8,128)} async-done(((f32[512,2048]{1,0:T(8,128)}), f32[512,2048]{1,0:T(8,128)}) %all-reduce.8.cloned.1.call-update) | async-done | bytes 4194320 | tf_op jit(solution)/shard_map/psum | solution.py:55
  278.1 45.8 %all-gather.14.cloned.1.call-done = bf16[2048,512]{1,0:T(8,128)(2,1)} async-done(((bf16[256,512]{1,0:T(8,128)(2,1)}), bf16[2048,512]{1,0:T(8,128)(2,1)}) %all-gather.14.cloned.1.call-update) | async-done | bytes 2097168 | tf_op jit(solution)/shard_map/all_gather | solution.py:141
  326.8 19.6 all-gather.12.cloned.1.call-done
  346.4 127.4 %all-gather.10.cloned.1.call-done = bf16[2,4096,512]{1,2,0:T(8,128)(2,1)} async-done(((bf16[2,512,512]{1,2,0:T(8,128)(2,1)}), bf16[2,4096,512]{1,2,0:T(8,128)(2,1)}) %all-gather.10.cloned.1.call-update) | async-done | bytes 8388624 | tf_op jit(solution)/shard_map/all_gather | solution.py:142
  481.7 42.6 %all-gather.16.cloned.1.call-done = bf16[512,2048]{1,0:T(8,128)(2,1)} async-done(((bf16[512,256]{1,0:T(8,128)(2,1)}), bf16[512,2048]{1,0:T(8,128)(2,1)}) %all-gather.16.cloned.1.call-update) | async-done | bytes 2097168 | tf_op jit(solution)/shard_map/all_gather | solution.py:143
  531.0 82.1 %all-reduce.10.cloned.1.call-done = f32[512,2048]{1,0:T(8,128)} async-done(((f32[512,2048]{1,0:T(8,128)}), f32[512,2048]{1,0:T(8,128)}) %all-reduce.10.cloned.1.call-update) | async-done | bytes 4194320 | tf_op jit(solution)/shard_map/psum | solution.py:55
  619.6 120.2 %all-gather.18.cloned.1.call-done = bf16[2048,2048]{1,0:T(8,128)(2,1)} async-done(((bf16[256,2048]{1,0:T(8,128)(2,1)}), bf16[2048,2048]{1,0:T(8,128)(2,1)}) %all-gather.18.cloned.1.call-update) | async-done | bytes 8388624 | tf_op jit(solution)/shard_map/all_gather | solution.py:144
  739.8 11.2 fusion.71
  751.0 114.0 %all-gather.20.cloned.1.call-done = bf16[2048,2048]{1,0:T(8,128)(2,1)} async-done(((bf16[2048,256]{1,0:T(8,128)(2,1)}), bf16[2048,2048]{1,0:T(8,128)(2,1)}) %all-gather.20.cloned.1.call-update) | async-done | bytes 8388624 | tf_op jit(solution)/shard_map/all_gather | solution.py:145
  865.0 11.6 fusion.70
  876.9 83.5 %all-reduce.12.cloned.1.call-done = f32[512,2048]{1,0:T(8,128)} async-done(((f32[512,2048]{1,0:T(8,128)}), f32[512,2048]{1,0:T(8,128)}) %all-reduce.12.cloned.1.call-update) | async-done | bytes 4194320 | tf_op jit(solution)/shard_map/psum | solution.py:55
  970.5 12.0 fusion.89
  990.4 85.2 %all-reduce.14.cloned.1.call-done = f32[512,2048]{1,0:T(8,128)} async-done(((f32[512,2048]{1,0:T(8,128)}), f32[512,2048]{1,0:T(8,128)}) %all-reduce.14.cloned.1.call-update) | async-done | bytes 4194320 | tf_op jit(solution)/shard_map/psum | solution.py:59
  1092.7 85.5 %all-reduce.16.cloned.1.call-done = f32[512,2048]{1,0:T(8,128)} async-done(((f32[512,2048]{1,0:T(8,128)}), f32[512,2048]{1,0:T(8,128)}) %all-reduce.16.cloned.1.call-update) | async-done | bytes 4194320 | tf_op jit(solution)/shard_map/psum | solution.py:59
  1239.4 12.4 convolution_convert_fusion
  1281.4 16.8 all-reduce.18.cloned.1.call-done
  1303.7 38.9 %all-reduce = (bf16[4,2048]{1,0:T(4,128)(2,1)S(1)}, bf16[4,2048]{1,0:T(4,128)(2,1)S(1)}, bf16[3,2048]{1,0:T(4,128)(2,1)S(1)}, bf16[2048]{0:T(1024)(128)(2,1)S(1)}) all-reduce(bf16[4,2048]{1,0:T(4,128)(2,1)S(1)} %get-tuple-element.218, bf16[4,2048]{1,0:T(4,128)(2,1)S(1)} %get-tuple-element.219, ...), channel_id=1, replica_groups=mesh['dp'=8,'mp'=4] {'dp'}, use_global_device_ids=true, to_apply=%region_40.41 | all-reduce | flops 24576 | bytes 98304 | tf_op jit(solution)/shard_map/psum | solution.py:278
  1350.7 20.3 reduce-scatter.15.cloned.1.call-done
  1372.8 31.3 %reduce-scatter.9.cloned.1.call-done = bf16[256,1024]{1,0:T(8,128)(2,1)} async-done(((bf16[256,4096]{1,0:T(8,128)(2,1)}), bf16[256,1024]{1,0:T(8,128)(2,1)}) %reduce-scatter.9.cloned.1.call-update) | async-done | bytes 524304 | tf_op jit(solution)/shard_map/reduce_scatter | solution.py:236
  1406.2 70.5 %reduce-scatter.19.cloned.1.call-done = bf16[512,256]{1,0:T(8,128)(2,1)} async-done(((bf16[512,2048]{1,0:T(8,128)(2,1)}), bf16[512,256]{1,0:T(8,128)(2,1)}) %reduce-scatter.19.cloned.1.call-update) | async-done | bytes 262160 | tf_op jit(solution)/shard_map/reduce_scatter | solution.py:296
  1478.5 70.4 %reduce-scatter.13.cloned.1.call-done = bf16[512,256]{1,0:T(8,128)(2,1)} async-done(((bf16[512,2048]{1,0:T(8,128)(2,1)}), bf16[512,256]{1,0:T(8,128)(2,1)}) %reduce-scatter.13.cloned.1.call-update) | async-done | bytes 262160 | tf_op jit(solution)/shard_map/reduce_scatter | solution.py:287
  1550.7 148.6 %reduce-scatter.23.cloned.1.call-done = bf16[2048,256]{1,0:T(8,128)(2,1)} async-done(((bf16[2048,2048]{1,0:T(8,128)(2,1)}), bf16[2048,256]{1,0:T(8,128)(2,1)}) %reduce-scatter.23.cloned.1.call-update) | async-done | bytes 1048592 | tf_op jit(solution)/shard_map/reduce_scatter | solution.py:302
  1702.0 147.5 %reduce-scatter.21.cloned.1.call-done = bf16[256,2048]{1,0:T(8,128)(2,1)} async-done(((bf16[2048,2048]{1,0:T(8,128)(2,1)}), bf16[256,2048]{1,0:T(8,128)(2,1)}) %reduce-scatter.21.cloned.1.call-update) | async-done | bytes 1048592 | tf_op jit(solution)/shard_map/reduce_scatter | solution.py:299
  1852.3 118.2 %reduce-scatter.11.cloned.1.call-done = bf16[3,256,512]{1,2,0:T(8,128)(2,1)} async-done(((bf16[3,2048,512]{1,2,0:T(8,128)(2,1)}), bf16[3,256,512]{1,2,0:T(8,128)(2,1)}) %reduce-scatter.11.cloned.1.call-update) | async-done | bytes 786448 | tf_op jit(solution)/shard_map/reduce_scatter | solution.py:284
  1973.1 148.2 %reduce-scatter.17.cloned.1.call-done = bf16[2,512,512]{1,2,0:T(8,128)(2,1)} async-done(((bf16[2,4096,512]{1,2,0:T(8,128)(2,1)}), bf16[2,512,512]{1,2,0:T(8,128)(2,1)}) %reduce-scatter.17.cloned.1.call-update) | async-done | bytes 1048592 | tf_op jit(solution)/shard_map/reduce_scatter | solution.py:293
  (291 shorter events, 230.8 us)
Async XLA Ops:
  7.2 177.3 %all-gather.8.cloned.1.call-start = ((), (), s32[]{:S(2)}) async-start(), calls=%async_computation.8 | async-start | bytes 2359296 | tf_op jit(solution)/shard_map/all_gather | solution.py:140
  7.3 23.8 %collective-permute-start = (bf16[3,256,512]{2,1,0:T(8,128)(2,1)}, bf16[3,256,512]{2,1,0:T(8,128)(2,1)S(1)}, u32[]{:S(2)}, u32[]{:S(2)}) collective-permute-start(bf16[3,256,512]{2,1,0:T(8,128)(2,1)} %param.20), channel_id=1, source_target_pairs={{0,4},{4,8},{8,12},{12,16},{16,20},{20,24},{24,28},{28,0},{1,5},{5... | collective-permute-start | bytes 2359304 | tf_op jit(solution)/shard_map/ppermute | solution.py:28
  31.1 27.6 %collective-permute-start.1 = (bf16[3,256,512]{2,1,0:T(8,128)(2,1)S(1)}, bf16[3,256,512]{2,1,0:T(8,128)(2,1)S(1)}, u32[]{:S(2)}, u32[]{:S(2)}) collective-permute-start(bf16[3,256,512]{2,1,0:T(8,128)(2,1)S(1)} %collective-permute-done), channel_id=1, source_target_pairs={{0,4},{4,8},{8,12},{12,16},{16,20},{20,24},{24,28},{28,0},{1,5},{5... | collective-permute-start | bytes 2359304 | tf_op jit(solution)/shard_map/ppermute | solution.py:28
  31.1 241.3 %all-reduce.8.cloned.1.call-start = ((), (), s32[]{:S(2)}) async-start(), calls=%async_computation.9 | async-start | bytes 8388608 | tf_op jit(solution)/shard_map/psum | solution.py:55
  58.7 19.4 collective-permute-start.2
  60.6 115.2 %copy-start.40 = (f32[512]{0:T(512)}, f32[512]{0:T(512)S(1)}, u32[]{:S(2)}) copy-start(f32[512]{0:T(512)S(1)} %broadcast_multiply_fusion.3) | copy-start | bytes 6148
  62.9 112.9 %copy-start.45 = (f32[512]{0:T(512)}, f32[512]{0:T(512)S(1)}, u32[]{:S(2)}) copy-start(f32[512]{0:T(512)S(1)} %fusion.58) | copy-start | bytes 6148
  78.1 36.7 %collective-permute-start.3 = (bf16[3,256,512]{2,1,0:T(8,128)(2,1)}, bf16[3,256,512]{2,1,0:T(8,128)(2,1)S(1)}, u32[]{:S(2)}, u32[]{:S(2)}) collective-permute-start(bf16[3,256,512]{2,1,0:T(8,128)(2,1)} %collective-permute-done.2), channel_id=1, source_target_pairs={{0,4},{4,8},{8,12},{12,16},{16,20},{20,24},{24,28},{28,0},{1,5},{5... | collective-permute-start | bytes 2359304 | tf_op jit(solution)/shard_map/ppermute | solution.py:28
  114.8 17.7 collective-permute-start.4
  132.5 17.7 collective-permute-start.5
  150.2 14.7 collective-permute-start.6
  190.2 133.7 %all-gather.14.cloned.1.call-start = ((), (), s32[]{:S(2)}) async-start(), calls=%async_computation.12 | async-start | bytes 2359296 | tf_op jit(solution)/shard_map/all_gather | solution.py:141
  190.9 155.5 %all-gather.12.cloned.1.call-start = ((), (), s32[]{:S(2)}) async-start(), calls=%async_computation.11 | async-start | bytes 2621440 | tf_op jit(solution)/shard_map/all_gather | solution.py:148
  191.5 282.4 %all-gather.10.cloned.1.call-start = ((), (), s32[]{:S(2)}) async-start(), calls=%async_computation.10 | async-start | bytes 9437184 | tf_op jit(solution)/shard_map/all_gather | solution.py:142
  192.9 331.4 %all-gather.16.cloned.1.call-start = ((), (), s32[]{:S(2)}) async-start(), calls=%async_computation.13 | async-start | bytes 2359296 | tf_op jit(solution)/shard_map/all_gather | solution.py:143
  193.5 419.5 %all-reduce.10.cloned.1.call-start = ((), (), s32[]{:S(2)}) async-start(), calls=%async_computation.14 | async-start | bytes 8388608 | tf_op jit(solution)/shard_map/psum | solution.py:55
  326.8 153.5 %copy-start.27 = (bf16[512,512]{0,1:T(8,128)(2,1)}, bf16[512,512]{0,1:T(8,128)(2,1)S(1)}, u32[]{:S(2)}) copy-start(bf16[512,512]{0,1:T(8,128)(2,1)S(1)} %convolution_convert_fusion.9) | copy-start | bytes 1572868
  529.2 210.6 %all-gather.18.cloned.1.call-start = ((), (), s32[]{:S(2)}) async-start(), calls=%async_computation.15 | async-start | bytes 9437184 | tf_op jit(solution)/shard_map/all_gather | solution.py:144
  530.0 335.0 %all-gather.20.cloned.1.call-start = ((), (), s32[]{:S(2)}) async-start(), calls=%async_computation.16 | async-start | bytes 9437184 | tf_op jit(solution)/shard_map/all_gather | solution.py:145
  530.7 429.7 %all-reduce.12.cloned.1.call-start = ((), (), s32[]{:S(2)}) async-start(), calls=%async_computation.17 | async-start | bytes 8388608 | tf_op jit(solution)/shard_map/psum | solution.py:55
  739.8 125.2 %copy-start.53 = (f32[2048]{0:T(1024)S(1)}, f32[2048]{0:T(1024)}, u32[]{:S(2)}) copy-start(f32[2048]{0:T(1024)} %param.30) | copy-start | bytes 24580
  876.6 199.1 %all-reduce.14.cloned.1.call-start = ((), (), s32[]{:S(2)}) async-start(), calls=%async_computation.18 | async-start | bytes 8388608 | tf_op jit(solution)/shard_map/psum | solution.py:59
  989.9 188.3 %all-reduce.16.cloned.1.call-start = ((), (), s32[]{:S(2)}) async-start(), calls=%async_computation.19 | async-start | bytes 8388608 | tf_op jit(solution)/shard_map/psum | solution.py:59
  1092.5 205.7 %all-reduce.18.cloned.1.call-start = ((), (), s32[]{:S(2)}) async-start(), calls=%async_computation.20 | async-start | bytes 8388608 | tf_op jit(solution)/shard_map/psum | solution.py:59
  1212.4 158.6 %reduce-scatter.15.cloned.1.call-start = ((), (), s32[]{:S(2)}) async-start(), calls=%async_computation.24 | async-start | bytes 2359296 | tf_op jit(solution)/shard_map/reduce_scatter | solution.py:290
  1216.8 187.3 %reduce-scatter.9.cloned.1.call-start = ((), (), s32[]{:S(2)}) async-start(), calls=%async_computation.21 | async-start | bytes 2621440 | tf_op jit(solution)/shard_map/reduce_scatter | solution.py:236
  1229.4 247.3 %reduce-scatter.19.cloned.1.call-start = ((), (), s32[]{:S(2)}) async-start(), calls=%async_computation.26 | async-start | bytes 2359296 | tf_op jit(solution)/shard_map/reduce_scatter | solution.py:296
  1234.4 314.5 %reduce-scatter.13.cloned.1.call-start = ((), (), s32[]{:S(2)}) async-start(), calls=%async_computation.23 | async-start | bytes 2359296 | tf_op jit(solution)/shard_map/reduce_scatter | solution.py:287
  1239.4 459.9 %reduce-scatter.23.cloned.1.call-start = ((), (), s32[]{:S(2)}) async-start(), calls=%async_computation.28 | async-start | bytes 9437184 | tf_op jit(solution)/shard_map/reduce_scatter | solution.py:302
  1251.8 597.6 %reduce-scatter.21.cloned.1.call-start = ((), (), s32[]{:S(2)}) async-start(), calls=%async_computation.27 | async-start | bytes 9437184 | tf_op jit(solution)/shard_map/reduce_scatter | solution.py:299
  1263.0 707.5 %reduce-scatter.11.cloned.1.call-start = ((), (), s32[]{:S(2)}) async-start(), calls=%async_computation.22 | async-start | bytes 7077888 | tf_op jit(solution)/shard_map/reduce_scatter | solution.py:284
  1272.0 849.3 %reduce-scatter.17.cloned.1.call-start = ((), (), s32[]{:S(2)}) async-start(), calls=%async_computation.25 | async-start | bytes 9437184 | tf_op jit(solution)/shard_map/reduce_scatter | solution.py:293
  (55 other events, 801.7 us)
Sparse Core Ops, SparseCore 0:
  31.3 81.3 all-gather.7
  190.3 82.1 all-reduce.7
  274.6 49.2 all-gather.13
  325.3 21.0 all-gather.11
  348.9 124.9 all-gather.9
  475.8 48.5 all-gather.15
  529.3 83.6 all-reduce.9
  615.1 124.6 all-gather.17
  741.8 123.1 all-gather.19
  876.7 83.6 all-reduce.11
  990.0 85.6 all-reduce.13
  1092.6 85.6 all-reduce.15
  1212.5 85.6 all-reduce.17
  1302.2 68.7 reduce-scatter.14
  1373.9 30.1 reduce-scatter.8
  1407.5 69.1 reduce-scatter.18
  1480.6 68.2 reduce-scatter.12
  1552.4 146.8 reduce-scatter.22
  1702.9 146.5 reduce-scatter.20
  1852.9 117.5 reduce-scatter.10
  1974.1 147.0 reduce-scatter.16
